TPU v7x, 256 devices: a whole 4x4x8 slice. The times are simulated.
256 devices in a mesh: row: 8 (over y, core), col: 8 (over x, z_hi), rep: 4 (over z_lo).
Axes of the slice: x: 4, y: 4, z: 8 (z_hi: 2, z_lo: 4; z = z_hi * 4 + z_lo), core: 2. Of those that a mesh axis runs over, the one named last changes fastest.
Arguments:
- features: float32 [256, 32768], P('rep', ('col', 'row')), may hold values from -6 to 6
- weight: float32 [256, 256], replicated, may hold values from -0.375 to 0.375
- cotangent: float32 [256, 32768], P('rep', ('row', 'col')), may hold values from -6 to 6
- tile_values: float32 [10240, 128, 128], P(('row', 'col')), may hold values from -0.078125 to 0.078125
- tile_row: int32 [10240], P(('row', 'col')), may hold values from 0 to 31
- tile_col: int32 [10240], P(('row', 'col')), may hold values from 0 to 31
- tile_kind: int32 [10240], P(('row', 'col')), may hold values from 0 to 159
- tile_count: int32 [64], P(('row', 'col')), may hold values from 40 to 160, as said below
Outputs:
- output: float32 [256, 32768], P('rep', ('row', 'col'))
- input_grad: float32 [256, 32768], P('rep', ('col', 'row'))
- weight_grad: float32 [256, 256], P('rep')
Inputs may be any that keep to these rules, and one draw needn't show every extreme that they name: `tile_count`: a block's slots at or after its count are not part of the adjacency; some block uses all 160 slots. `tile_row`: slots may repeat a tile position; their tiles add. `tile_kind`: an index into the 160 stored tiles of the same block.
All inputs are finite; a program needn't handle non-finite values.
Results may differ from a plain program's by a relative error of at most 0.0001.
Values sent between devices are 32-bit elements; how exact they have to be, the bound alone decides.
No kernel may reach another device: no remote copies, remote signals or barrier semaphores. Data moves between devices by JAX's collectives and lax.ppermute only.
A program may use at most 128 MiB of HBM per device.

v0:
```python
import jax
import jax.numpy as jnp
from jax import lax
from jax.sharding import PartitionSpec as P


def tile_terms(source, values, from_tile, to_tile, tile_kinds, live_weight, dest_tiles, transposed):
    feat_width = source.shape[0]
    tile_edge = values.shape[1]
    tiled = source.reshape(feat_width, source.shape[1] // tile_edge, tile_edge)
    picked = jnp.take(tiled, from_tile, axis=1)
    chosen = jnp.take(values, tile_kinds, axis=0)
    if transposed:
        products = jnp.einsum("fga,gab->fgb", picked, chosen, precision=lax.Precision.HIGHEST)
    else:
        products = jnp.einsum("fgb,gab->fga", picked, chosen, precision=lax.Precision.HIGHEST)
    onehot = (to_tile[:, None] == jnp.arange(dest_tiles, dtype=jnp.int32)[None, :]).astype(
        jnp.float32
    )
    onehot = onehot * live_weight[:, None]
    spread = jnp.einsum("fgt,gd->fdt", products, onehot, precision=lax.Precision.HIGHEST)
    return spread.reshape(feat_width, dest_tiles * tile_edge)


def aggregate(source, values, from_tile, to_tile, tile_kinds, live_count, dest_tiles, transposed):
    slot_total = tile_kinds.shape[0]
    live_weight = (jnp.arange(slot_total, dtype=jnp.int32) < live_count).astype(jnp.float32)
    return tile_terms(
        source, values, from_tile, to_tile, tile_kinds, live_weight, dest_tiles, transposed
    )


def local(features, weight, cotangent, tile_values, tile_row, tile_col, tile_kind, tile_count):
    n_rowdev = lax.axis_size("row")
    n_coldev = lax.axis_size("col")
    n_repdev = lax.axis_size("rep")
    quarter = weight.shape[0] // n_repdev
    rep_index = lax.axis_index("rep")
    own_rows = lax.dynamic_slice_in_dim(weight, rep_index * quarter, quarter, 0)
    own_cols = lax.dynamic_slice_in_dim(weight, rep_index * quarter, quarter, 1)
    stretch_len = features.shape[1]
    tile_edge = tile_values.shape[1]
    live_count = tile_count[0]
    row_tiles = n_coldev * stretch_len // tile_edge
    col_tiles = n_rowdev * stretch_len // tile_edge
    mixed = lax.psum_scatter(
        lax.dot_general(
            own_rows,
            features,
            (((0,), (0,)), ((), ())),
            precision=lax.Precision.HIGHEST,
            preferred_element_type=jnp.float32,
        ),
        "rep",
        scatter_dimension=0,
        tiled=True,
    )
    column_block = lax.all_gather(mixed, "row", axis=1, tiled=True)
    partial_value = aggregate(
        column_block, tile_values, tile_col, tile_row, tile_kind, live_count, row_tiles, False
    )
    summed = lax.psum_scatter(partial_value, "col", scatter_dimension=1, tiled=True)
    output, pullback = jax.vjp(lambda v: jax.nn.gelu(v, approximate=True), summed)
    (grad_pre,) = pullback(cotangent)
    row_block = lax.all_gather(grad_pre, "col", axis=1, tiled=True)
    partial_back = aggregate(
        row_block, tile_values, tile_row, tile_col, tile_kind, live_count, col_tiles, True
    )
    grad_mixed = lax.psum_scatter(partial_back, "row", scatter_dimension=1, tiled=True)
    input_grad = lax.psum_scatter(
        jnp.dot(
            own_cols,
            grad_mixed,
            preferred_element_type=jnp.float32,
            precision=lax.Precision.HIGHEST,
        ),
        "rep",
        scatter_dimension=0,
        tiled=True,
    )
    weight_part = lax.dot_general(
        features,
        lax.all_gather(grad_mixed, "rep", axis=0, tiled=True),
        (((1,), (1,)), ((), ())),
        precision=lax.Precision.HIGHEST,
        preferred_element_type=jnp.float32,
    )
    node_total = stretch_len * n_rowdev * n_coldev
    weight_grad = lax.psum(weight_part * float(node_total) ** (-0.5), ("row", "col"))
    return (output, input_grad, weight_grad)


def solution(mesh):
    return jax.shard_map(
        local,
        mesh=mesh,
        in_specs=(
            P("rep", ("col", "row")),
            P(),
            P("rep", ("row", "col")),
            P(("row", "col"), None, None),
            P(("row", "col")),
            P(("row", "col")),
            P(("row", "col")),
            P(("row", "col")),
        ),
        out_specs=(P("rep", ("row", "col")), P("rep", ("col", "row")), P("rep", None)),
        check_vma=False,
    )
```

profile of v0, /device:TPU:2, one launch (start us, length us, event | category | flops | bytes accessed | tf_op | source)
XLA Modules:
  0.0 1082.4 jit_solution(2901445615518222513)
XLA Ops:
  7.2 0.0 copy-start
  7.2 0.0 reduce-scatter.5.cloned.1.call-start
  7.2 0.9 copy-done
  8.1 2.3 fusion.39
  10.4 0.0 reduce-scatter.5.cloned.1.call-update
  10.5 0.0 all-gather.3.cloned.1.call-start
  10.5 30.2 %reduce-scatter.5.cloned.1.call-done = f32[64,512]{1,0:T(8,128)} async-done(((f32[256,512]{1,0:T(8,128)}), f32[64,512]{1,0:T(8,128)}) %reduce-scatter.5.cloned.1.call-update) | async-done | bytes 131088 | tf_op jit(solution)/shard_map/reduce_scatter | solution.py:46
  40.7 0.0 all-gather.3.cloned.1.call-update
  40.7 0.0 reduce-scatter.7.cloned.1.call-start
  41.4 0.7 compare_select_fusion.2
  42.1 0.0 copy-start.3
  42.1 0.0 copy-start.5
  42.1 14.2 %gather_fusion = f32[160,128,128]{2,1,0:T(8,128)} fusion(f32[160,128,128]{2,1,0:T(8,128)} %param.15, s32[1024]{0:T(1024)S(1)} %pad_clamp_fusion.2), kind=kCustom, calls=%fused_computation.clone | custom fusion | bytes 20972160 | tf_op jit(solution)/shard_map/jit(_take)/gather | solution.py:12
  56.3 0.0 copy-done.3
  56.3 0.0 copy-done.5
  56.3 10.5 all-gather.3.cloned.1.call-done
  66.8 1.3 copy_bitcast_fusion.3
  68.2 3.3 gather_fusion.1
  71.5 0.0 copy-start.4
  71.5 24.3 %fusion.20 = f32[64,160,128]{2,0,1:T(8,128)S(1)} fusion(f32[160,64,128]{2,1,0:T(8,128)} %gather_fusion.1, pred[160]{0:T(512)(128)(4,1)S(1)} %get-tuple-element.7, f32[160,128,128]{2,1,0:T(8,128)} %gather_fusion, pred[160]{0:T(512)(128)(4,1)S(1)} %get-tuple-element.8), kind=kOutput, calls=%fused_computation.23 | convolution fusion | flops 2017198080 | bytes 20971840 | tf_op jit(solution)/shard_map/fgb,gab->fga/dot_general | solution.py:16
  95.8 0.0 copy-done.4
  95.8 0.0 copy-start.2
  95.8 5.6 fusion.8
  101.5 1.6 copy.29
  103.0 0.0 reduce-scatter.7.cloned.1.call-update
  103.1 0.0 all-gather.5.cloned.1.call-start
  103.1 87.2 %reduce-scatter.7.cloned.1.call-done = f32[64,512]{1,0:T(8,128)} async-done(((f32[64,4096]{1,0:T(8,128)}), f32[64,512]{1,0:T(8,128)}) %reduce-scatter.7.cloned.1.call-update) | async-done | bytes 131088 | tf_op jit(solution)/shard_map/reduce_scatter | solution.py:62
  190.4 0.0 copy-done.2
  190.4 1.7 fusion.36
  192.1 0.0 all-gather.5.cloned.1.call-update
  192.1 0.0 reduce-scatter.9.cloned.1.call-start
  192.2 59.1 %all-gather.5.cloned.1.call-done = f32[64,4096]{1,0:T(8,128)} async-done(((f32[64,512]{1,0:T(8,128)}), f32[64,4096]{1,0:T(8,128)}) %all-gather.5.cloned.1.call-update) | async-done | bytes 1048592 | tf_op jit(solution)/shard_map/all_gather | solution.py:65
  251.3 1.3 copy_bitcast_fusion.2
  252.7 3.3 gather_fusion.2
  255.9 13.9 %fusion.25 = f32[64,160,128]{2,0,1:T(8,128)S(1)} fusion(f32[160,64,128]{2,1,0:T(8,128)} %gather_fusion.2, pred[160]{0:T(512)(128)(4,1)S(1)} %compare_and_fusion, f32[160,128,128]{2,1,0:T(8,128)} %gather_fusion, pred[160]{0:T(512)(128)(4,1)S(1)} %get-tuple-element.8), kind=kOutput, calls=%fused_computation.24 | convolution fusion | flops 2017198080 | bytes 20971840 | tf_op jit(solution)/shard_map/fga,gab->fgb/dot_general | solution.py:14
  269.8 0.0 copy-start.1
  269.8 5.6 fusion.6
  275.5 1.6 copy.28
  277.1 0.0 reduce-scatter.9.cloned.1.call-update
  277.1 0.0 all-reduce.2.cloned.1.call-start
  277.1 30.8 %reduce-scatter.9.cloned.1.call-done = f32[64,512]{1,0:T(8,128)} async-done(((f32[64,4096]{1,0:T(8,128)}), f32[64,512]{1,0:T(8,128)}) %reduce-scatter.9.cloned.1.call-update) | async-done | bytes 131088 | tf_op jit(solution)/shard_map/reduce_scatter | solution.py:69
  307.9 16.4 %all_gather.11 = f32[256,512]{1,0:T(8,128)S(1)} all-gather(f32[64,512]{1,0:T(8,128)} %reduce-scatter.9.cloned.1.call-done), channel_id=1, replica_groups=mesh['row'=8,'col'=8,'rep'=4] {'rep'}, dimensions={0}, use_global_device_ids=true | all-gather | bytes 655360 | tf_op jit(solution)/shard_map/all_gather | solution.py:83
  324.4 0.0 copy-done.1
  324.4 1.2 fusion.30
  325.6 0.0 all-reduce.2.cloned.1.call-update
  325.6 0.0 reduce-scatter.11.cloned.1.call-start
  325.7 2.3 fusion.37
  328.0 0.0 reduce-scatter.11.cloned.1.call-update
  328.0 722.2 %all-reduce.2.cloned.1.call-done = f32[64,256]{1,0:T(8,128)} async-done(((f32[64,256]{1,0:T(8,128)}), f32[64,256]{1,0:T(8,128)}) %all-reduce.2.cloned.1.call-update) | async-done | bytes 65552 | tf_op jit(solution)/shard_map/psum | solution.py:89
  1050.2 23.9 %reduce-scatter.11.cloned.1.call-done = f32[64,512]{1,0:T(8,128)} async-done(((f32[256,512]{1,0:T(8,128)}), f32[64,512]{1,0:T(8,128)}) %reduce-scatter.11.cloned.1.call-update) | async-done | bytes 131088 | tf_op jit(solution)/shard_map/reduce_scatter | solution.py:70
  1074.1 1.5 copy.32
  (8 shorter events, 0.0 us)
Async XLA Ops:
  7.2 1.0 copy-start
  7.2 33.5 %reduce-scatter.5.cloned.1.call-start = ((), (), s32[]{:S(2)}) async-start(), calls=%async_computation.4 | async-start | bytes 655360 | tf_op jit(solution)/shard_map/reduce_scatter | solution.py:46
  10.5 56.4 %all-gather.3.cloned.1.call-start = ((), (), s32[]{:S(2)}) async-start(), calls=%async_computation.5 | async-start | bytes 1179648 | tf_op jit(solution)/shard_map/all_gather | solution.py:58
  40.7 149.7 %reduce-scatter.7.cloned.1.call-start = ((), (), s32[]{:S(2)}) async-start(), calls=%async_computation.6 | async-start | bytes 1179648 | tf_op jit(solution)/shard_map/reduce_scatter | solution.py:62
  42.1 14.2 %copy-start.3 = (s32[160]{0:T(256)S(1)}, s32[160]{0:T(256)}, u32[]{:S(2)}) copy-start(s32[160]{0:T(256)} %param.17) | copy-start | bytes 1924
  42.1 14.2 %copy-start.5 = (s32[160]{0:T(256)S(1)}, s32[160]{0:T(256)}, u32[]{:S(2)}) copy-start(s32[160]{0:T(256)} %param.18) | copy-start | bytes 1924
  71.5 24.3 %copy-start.4 = (s32[160]{0:T(256)S(1)}, s32[160]{0:T(256)}, u32[]{:S(2)}) copy-start(s32[160]{0:T(256)} %param.16) | copy-start | bytes 1924
  95.8 94.6 %copy-start.2 = (f32[64,512]{1,0:T(8,128)S(1)}, f32[64,512]{1,0:T(8,128)}, u32[]{:S(2)}) copy-start(f32[64,512]{1,0:T(8,128)} %param.14) | copy-start | bytes 393220
  103.1 148.2 %all-gather.5.cloned.1.call-start = ((), (), s32[]{:S(2)}) async-start(), calls=%async_computation.7 | async-start | bytes 1179648 | tf_op jit(solution)/shard_map/all_gather | solution.py:65
  192.1 115.8 %reduce-scatter.9.cloned.1.call-start = ((), (), s32[]{:S(2)}) async-start(), calls=%async_computation.8 | async-start | bytes 1179648 | tf_op jit(solution)/shard_map/reduce_scatter | solution.py:69
  269.8 54.5 %copy-start.1 = (f32[64,512]{1,0:T(8,128)S(1)}, f32[64,512]{1,0:T(8,128)}, u32[]{:S(2)}) copy-start(f32[64,512]{1,0:T(8,128)} %param.12) | copy-start | bytes 393220
  277.1 773.1 %all-reduce.2.cloned.1.call-start = ((), (), s32[]{:S(2)}) async-start(), calls=%async_computation.10 | async-start | bytes 131072 | tf_op jit(solution)/shard_map/psum | solution.py:89
  325.6 748.5 %reduce-scatter.11.cloned.1.call-start = ((), (), s32[]{:S(2)}) async-start(), calls=%async_computation.9 | async-start | bytes 655360 | tf_op jit(solution)/shard_map/reduce_scatter | solution.py:70
Sparse Core Ops, SparseCore 0:
  10.6 30.0 reduce-scatter.4
  42.5 24.2 all-gather.2
  103.2 87.1 reduce-scatter.6
  193.4 57.8 all-gather.4
  277.2 30.6 reduce-scatter.8
  325.7 724.4 all-reduce.1
  1053.3 20.7 reduce-scatter.10
where the time goes:
time: 1080 us
  waiting for transfers between devices  964 us (89%)
  matrix products  55.3 us (5%)
  local copies, waits for them, and re-layouts  29 us (3%)
  blocking collectives  16.4 us (2%)
  between operations  14.9 us (1%)
    psum x1, waiting for transfers between devices, local(): lax.psum(weight_part * float(node_total) ** (-0.5), ('row', 'col'))  722 us
    reduce_scatter x1, waiting for transfers between devices, local(): lax.psum_scatter(partial_value, 'col', scatter_dimension=1, tiled=True)  87.2 us
    all_gather x1, waiting for transfers between devices, local(): row_block = lax.all_gather(grad_pre, 'col', axis=1, tiled=True)  59.1 us
    reduce_scatter x1, waiting for transfers between devices, local(): lax.psum_scatter(partial_back, 'row', scatter_dimension=1, tiled=True)  30.8 us
    reduce_scatter x1, waiting for transfers between devices, local(): lax.psum_scatter(lax.dot_general(own_rows, features, (((0,), (0,)), ((),...  30.2 us
    dot_general x1, matrix products, tile_terms(): jnp.einsum('fgb,gab->fga', picked, chosen, precision=lax.Precision.HIGHEST)  24.3 us
    reduce_scatter x1, waiting for transfers between devices, local(): lax.psum_scatter(jnp.dot(own_cols, grad_mixed, preferred_element_type=jnp...  23.9 us
  transfers between devices with their start and end apart: 7, of which 7 were waited for; matrix products, arithmetic and copies ran while one was open for 2% of the time, Pallas kernels for 0%

commit v1 on v0

--- a/solution.py
+++ b/solution.py
@@ -86,7 +86,7 @@
         preferred_element_type=jnp.float32,
     )
     node_total = stretch_len * n_rowdev * n_coldev
-    weight_grad = lax.psum(weight_part * float(node_total) ** (-0.5), ("row", "col"))
+    weight_grad = lax.psum(lax.psum(weight_part * float(node_total) ** (-0.5), "col"), "row")
     return (output, input_grad, weight_grad)
 
 

time: 1080 us -> 529 us (0.49)
  waiting for transfers between devices: 964 us -> 411 us
    psum x1 -> x2, waiting for transfers between devices: 722 us -> 163 us  [the longest x1 102 us: local(): lax.psum(weight_part * float(node_total) ** (-0.5), 'col')]
  transfers between devices with their start and end apart: 7 -> 8, of which waited for: 7 -> 8; matrix products, arithmetic and copies ran while one was open for 2% -> 3% of each run, Pallas kernels for 0% -> 0%
where the time goes in v1:
time: 529 us
  waiting for transfers between devices  411 us (78%)
  matrix products  55.3 us (10%)
  local copies, waits for them, and re-layouts  29 us (5%)
  blocking collectives  16.4 us (3%)
  between operations  14.9 us (3%)
    psum x1, waiting for transfers between devices, local(): lax.psum(weight_part * float(node_total) ** (-0.5), 'col')  102 us
    reduce_scatter x1, waiting for transfers between devices, local(): lax.psum_scatter(partial_value, 'col', scatter_dimension=1, tiled=True)  87.2 us
    psum x1, waiting for transfers between devices, local(): lax.psum(lax.psum(weight_part * float(node_total) ** (-0.5), 'col'), 'row')  61 us
    all_gather x1, waiting for transfers between devices, local(): row_block = lax.all_gather(grad_pre, 'col', axis=1, tiled=True)  59.1 us
    reduce_scatter x1, waiting for transfers between devices, local(): lax.psum_scatter(partial_back, 'row', scatter_dimension=1, tiled=True)  30.8 us
    reduce_scatter x1, waiting for transfers between devices, local(): lax.psum_scatter(lax.dot_general(own_rows, features, (((0,), (0,)), ((),...  30.2 us
    reduce_scatter x1, waiting for transfers between devices, local(): lax.psum_scatter(jnp.dot(own_cols, grad_mixed, preferred_element_type=jnp...  29.2 us
    dot_general x1, matrix products, tile_terms(): jnp.einsum('fgb,gab->fga', picked, chosen, precision=lax.Precision.HIGHEST)  24.3 us
  transfers between devices with their start and end apart: 8, of which 8 were waited for; matrix products, arithmetic and copies ran while one was open for 3% of the time, Pallas kernels for 0%

profile of v1, /device:TPU:2, one launch (start us, length us, event | category | flops | bytes accessed | tf_op | source)
XLA Modules:
  0.0 529.0 jit_solution(12148352572495384220)
XLA Ops:
  7.2 0.0 copy-start
  7.2 0.0 reduce-scatter.5.cloned.1.call-start
  7.2 0.9 copy-done
  8.1 2.3 fusion.39
  10.4 0.0 reduce-scatter.5.cloned.1.call-update
  10.5 0.0 all-gather.3.cloned.1.call-start
  10.5 30.2 %reduce-scatter.5.cloned.1.call-done = f32[64,512]{1,0:T(8,128)} async-done(((f32[256,512]{1,0:T(8,128)}), f32[64,512]{1,0:T(8,128)}) %reduce-scatter.5.cloned.1.call-update) | async-done | bytes 131088 | tf_op jit(solution)/shard_map/reduce_scatter | solution.py:46
  40.7 0.0 all-gather.3.cloned.1.call-update
  40.7 0.0 reduce-scatter.7.cloned.1.call-start
  41.4 0.7 compare_select_fusion.2
  42.1 0.0 copy-start.3
  42.1 0.0 copy-start.5
  42.1 14.2 %gather_fusion = f32[160,128,128]{2,1,0:T(8,128)} fusion(f32[160,128,128]{2,1,0:T(8,128)} %param.15, s32[1024]{0:T(1024)S(1)} %pad_clamp_fusion.2), kind=kCustom, calls=%fused_computation.clone | custom fusion | bytes 20972160 | tf_op jit(solution)/shard_map/jit(_take)/gather | solution.py:12
  56.3 0.0 copy-done.3
  56.3 0.0 copy-done.5
  56.3 10.5 %all-gather.3.cloned.1.call-done = f32[64,4096]{1,0:T(8,128)} async-done(((f32[64,512]{1,0:T(8,128)}), f32[64,4096]{1,0:T(8,128)}) %all-gather.3.cloned.1.call-update) | async-done | bytes 1048592 | tf_op jit(solution)/shard_map/all_gather | solution.py:58
  66.8 1.3 copy_bitcast_fusion.3
  68.2 3.3 gather_fusion.1
  71.5 0.0 copy-start.4
  71.5 24.3 %fusion.20 = f32[64,160,128]{2,0,1:T(8,128)S(1)} fusion(f32[160,64,128]{2,1,0:T(8,128)} %gather_fusion.1, pred[160]{0:T(512)(128)(4,1)S(1)} %get-tuple-element.7, f32[160,128,128]{2,1,0:T(8,128)} %gather_fusion, pred[160]{0:T(512)(128)(4,1)S(1)} %get-tuple-element.8), kind=kOutput, calls=%fused_computation.23 | convolution fusion | flops 2017198080 | bytes 20971840 | tf_op jit(solution)/shard_map/fgb,gab->fga/dot_general | solution.py:16
  95.8 0.0 copy-done.4
  95.8 0.0 copy-start.2
  95.8 5.6 %fusion.8 = f32[32,64,128]{2,0,1:T(8,128)S(1)} fusion(f32[64,160,128]{2,0,1:T(8,128)S(1)} %fusion.20, f32[160]{0:T(256)S(1)} %compare_convert_fusion, s32[160]{0:T(256)S(1)} %copy-done.4), kind=kOutput, calls=%fused_computation.11 | convolution fusion | flops 503326720 | bytes 6292736 | tf_op jit(solution)/shard_map/fgt,gd->fdt/dot_general | solution.py:21
  101.5 1.6 copy.29
  103.0 0.0 reduce-scatter.7.cloned.1.call-update
  103.1 0.0 all-gather.5.cloned.1.call-start
  103.1 87.2 %reduce-scatter.7.cloned.1.call-done = f32[64,512]{1,0:T(8,128)} async-done(((f32[64,4096]{1,0:T(8,128)}), f32[64,512]{1,0:T(8,128)}) %reduce-scatter.7.cloned.1.call-update) | async-done | bytes 131088 | tf_op jit(solution)/shard_map/reduce_scatter | solution.py:62
  190.4 0.0 copy-done.2
  190.4 1.7 fusion.36
  192.1 0.0 all-gather.5.cloned.1.call-update
  192.1 0.0 reduce-scatter.9.cloned.1.call-start
  192.2 59.1 %all-gather.5.cloned.1.call-done = f32[64,4096]{1,0:T(8,128)} async-done(((f32[64,512]{1,0:T(8,128)}), f32[64,4096]{1,0:T(8,128)}) %all-gather.5.cloned.1.call-update) | async-done | bytes 1048592 | tf_op jit(solution)/shard_map/all_gather | solution.py:65
  251.3 1.3 copy_bitcast_fusion.2
  252.7 3.3 gather_fusion.2
  255.9 13.9 %fusion.25 = f32[64,160,128]{2,0,1:T(8,128)S(1)} fusion(f32[160,64,128]{2,1,0:T(8,128)} %gather_fusion.2, pred[160]{0:T(512)(128)(4,1)S(1)} %compare_and_fusion, f32[160,128,128]{2,1,0:T(8,128)} %gather_fusion, pred[160]{0:T(512)(128)(4,1)S(1)} %get-tuple-element.8), kind=kOutput, calls=%fused_computation.24 | convolution fusion | flops 2017198080 | bytes 20971840 | tf_op jit(solution)/shard_map/fga,gab->fgb/dot_general | solution.py:14
  269.8 0.0 copy-start.1
  269.8 5.6 %fusion.6 = f32[32,64,128]{2,0,1:T(8,128)S(1)} fusion(f32[64,160,128]{2,0,1:T(8,128)S(1)} %fusion.25, s32[160]{0:T(256)S(1)} %copy-done.3, f32[160]{0:T(256)S(1)} %compare_convert_fusion), kind=kOutput, calls=%fused_computation.9 | convolution fusion | flops 503326720 | bytes 6292736 | tf_op jit(solution)/shard_map/fgt,gd->fdt/dot_general | solution.py:21
  275.5 1.6 copy.28
  277.1 0.0 reduce-scatter.9.cloned.1.call-update
  277.1 0.0 all-reduce.3.cloned.1.call-start
  277.1 30.8 %reduce-scatter.9.cloned.1.call-done = f32[64,512]{1,0:T(8,128)} async-done(((f32[64,4096]{1,0:T(8,128)}), f32[64,512]{1,0:T(8,128)}) %reduce-scatter.9.cloned.1.call-update) | async-done | bytes 131088 | tf_op jit(solution)/shard_map/reduce_scatter | solution.py:69
  307.9 16.4 %all_gather.11 = f32[256,512]{1,0:T(8,128)S(1)} all-gather(f32[64,512]{1,0:T(8,128)} %reduce-scatter.9.cloned.1.call-done), channel_id=1, replica_groups=mesh['row'=8,'col'=8,'rep'=4] {'rep'}, dimensions={0}, use_global_device_ids=true | all-gather | bytes 655360 | tf_op jit(solution)/shard_map/all_gather | solution.py:83
  324.4 0.0 copy-done.1
  324.4 1.2 fusion.30
  325.6 0.0 all-reduce.3.cloned.1.call-update
  325.6 0.0 all-reduce.5.cloned.1.call-start
  325.7 102.4 %all-reduce.3.cloned.1.call-done = f32[64,256]{1,0:T(8,128)} async-done(((f32[64,256]{1,0:T(8,128)}), f32[64,256]{1,0:T(8,128)}) %all-reduce.3.cloned.1.call-update) | async-done | bytes 65552 | tf_op jit(solution)/shard_map/psum | solution.py:89
  428.1 0.0 all-reduce.5.cloned.1.call-update
  428.1 0.0 reduce-scatter.11.cloned.1.call-start
  428.1 2.3 fusion.37
  430.5 0.0 reduce-scatter.11.cloned.1.call-update
  430.5 61.0 %all-reduce.5.cloned.1.call-done = f32[64,256]{1,0:T(8,128)} async-done(((f32[64,256]{1,0:T(8,128)}), f32[64,256]{1,0:T(8,128)}) %all-reduce.5.cloned.1.call-update) | async-done | bytes 65552 | tf_op jit(solution)/shard_map/psum | solution.py:89
  491.5 29.2 %reduce-scatter.11.cloned.1.call-done = f32[64,512]{1,0:T(8,128)} async-done(((f32[256,512]{1,0:T(8,128)}), f32[64,512]{1,0:T(8,128)}) %reduce-scatter.11.cloned.1.call-update) | async-done | bytes 131088 | tf_op jit(solution)/shard_map/reduce_scatter | solution.py:70
  520.7 1.5 copy.33
  (8 shorter events, 0.0 us)
Async XLA Ops:
  7.2 1.0 copy-start
  7.2 33.5 %reduce-scatter.5.cloned.1.call-start = ((), (), s32[]{:S(2)}) async-start(), calls=%async_computation.4 | async-start | bytes 655360 | tf_op jit(solution)/shard_map/reduce_scatter | solution.py:46
  10.5 56.4 %all-gather.3.cloned.1.call-start = ((), (), s32[]{:S(2)}) async-start(), calls=%async_computation.5 | async-start | bytes 1179648 | tf_op jit(solution)/shard_map/all_gather | solution.py:58
  40.7 149.7 %reduce-scatter.7.cloned.1.call-start = ((), (), s32[]{:S(2)}) async-start(), calls=%async_computation.6 | async-start | bytes 1179648 | tf_op jit(solution)/shard_map/reduce_scatter | solution.py:62
  42.1 14.2 %copy-start.3 = (s32[160]{0:T(256)S(1)}, s32[160]{0:T(256)}, u32[]{:S(2)}) copy-start(s32[160]{0:T(256)} %param.17) | copy-start | bytes 1924
  42.1 14.2 %copy-start.5 = (s32[160]{0:T(256)S(1)}, s32[160]{0:T(256)}, u32[]{:S(2)}) copy-start(s32[160]{0:T(256)} %param.18) | copy-start | bytes 1924
  71.5 24.3 %copy-start.4 = (s32[160]{0:T(256)S(1)}, s32[160]{0:T(256)}, u32[]{:S(2)}) copy-start(s32[160]{0:T(256)} %param.16) | copy-start | bytes 1924
  95.8 94.6 %copy-start.2 = (f32[64,512]{1,0:T(8,128)S(1)}, f32[64,512]{1,0:T(8,128)}, u32[]{:S(2)}) copy-start(f32[64,512]{1,0:T(8,128)} %param.14) | copy-start | bytes 393220
  103.1 148.2 %all-gather.5.cloned.1.call-start = ((), (), s32[]{:S(2)}) async-start(), calls=%async_computation.7 | async-start | bytes 1179648 | tf_op jit(solution)/shard_map/all_gather | solution.py:65
  192.1 115.8 %reduce-scatter.9.cloned.1.call-start = ((), (), s32[]{:S(2)}) async-start(), calls=%async_computation.8 | async-start | bytes 1179648 | tf_op jit(solution)/shard_map/reduce_scatter | solution.py:69
  269.8 54.5 %copy-start.1 = (f32[64,512]{1,0:T(8,128)S(1)}, f32[64,512]{1,0:T(8,128)}, u32[]{:S(2)}) copy-start(f32[64,512]{1,0:T(8,128)} %param.12) | copy-start | bytes 393220
  277.1 151.0 %all-reduce.3.cloned.1.call-start = ((), (), s32[]{:S(2)}) async-start(), calls=%async_computation.10 | async-start | bytes 131072 | tf_op jit(solution)/shard_map/psum | solution.py:89
  325.6 165.9 %all-reduce.5.cloned.1.call-start = ((), (), s32[]{:S(2)}) async-start(), calls=%async_computation.11 | async-start | bytes 131072 | tf_op jit(solution)/shard_map/psum | solution.py:89
  428.1 92.6 %reduce-scatter.11.cloned.1.call-start = ((), (), s32[]{:S(2)}) async-start(), calls=%async_computation.9 | async-start | bytes 655360 | tf_op jit(solution)/shard_map/reduce_scatter | solution.py:70
Sparse Core Ops, SparseCore 0:
  10.6 30.0 reduce-scatter.4
  42.5 24.2 all-gather.2
  103.2 87.1 reduce-scatter.6
  193.4 57.8 all-gather.4
  277.2 30.6 reduce-scatter.8
  325.7 102.2 all-reduce.2
  430.4 61.0 all-reduce.4
  494.6 26.0 reduce-scatter.10
